TPU v7x, 32 devices: a whole 2x2x4 slice. The times are simulated.
32 devices in a mesh: grp: 2 (over y), smp: 4 (over z), mrk: 4 (over x, core).
Axes of the slice: x: 2, y: 2, z: 4, core: 2. Of those that a mesh axis runs over, the one named last changes fastest.
Arguments:
- genotypes: bfloat16 [4096, 16384], P('smp', ('grp', 'mrk')), parts along dimension 1, may hold values from 0 to 2, as said below
- effect_class: int32 [16384], P(('grp', 'mrk')), parts along dimension 0, may hold values from 0 to 511
- effect_table: bfloat16 [1024, 256], P('grp'), parts along dimension 0, may hold values from -0.0625 to 0.0625
Outputs:
- assoc: float32 [256, 16384], P('smp', ('grp', 'mrk')), parts along dimension 1
There are 2 independent parts, one for each index of `grp`. A program takes and returns all parts, laid end to end along the dimension named above; each array names one. Nothing has to cross between parts.
Inputs may be any that keep to these rules, and one draw needn't show every extreme that they name: `genotypes`: dosages are whole numbers.
All inputs are finite; a program needn't handle non-finite values.
Results may differ from a plain program's by a relative error of at most 0.0032.
Values may be sent and summed in bfloat16 or wider, within the bound.
No kernel may reach another device: no remote copies, remote signals or barrier semaphores. Data moves between devices by JAX's collectives and lax.ppermute only.
A program may use at most 64 MiB of HBM per device.

v0:
```python
import math
import jax
import jax.numpy as jnp
from jax import lax
from jax.sharding import PartitionSpec as P

BLK_DEV = 1024
NBLK = 2
EPSILON = 1e-05


def marker_moments(genotypes, samples):
    totals = jnp.sum(genotypes, axis=0, dtype=jnp.float32)
    center = lax.psum(totals, "smp") / samples
    local_squares = jnp.sum(jnp.square(genotypes.astype(jnp.float32) - center[None, :]), axis=0)
    spread = lax.psum(local_squares, "smp") / samples
    return lax.rsqrt(spread + EPSILON)


def standardize(phenotype, samples):
    totals = jnp.sum(phenotype, axis=0)
    center = lax.psum(totals, "smp") / samples
    local_squares = jnp.sum(jnp.square(phenotype - center[None, :]), axis=0)
    spread = lax.psum(local_squares, "smp") / samples
    return ((phenotype - center[None, :]) * lax.rsqrt(spread + EPSILON)[None, :]).astype(
        jnp.bfloat16
    )


def shards(genotypes, effect_class, effect_table):
    samples = genotypes.shape[0] * lax.axis_size("smp")
    markers_here = genotypes.shape[1]
    inverse_spread = marker_moments(genotypes, samples)
    classes_iota = lax.broadcasted_iota(jnp.int32, (markers_here, effect_table.shape[0]), 1)
    onehot = (effect_class[:, None] == classes_iota).astype(jnp.bfloat16)
    effects = jnp.dot(onehot, effect_table, preferred_element_type=jnp.float32)
    scaled = (effects * inverse_spread[:, None]).astype(jnp.bfloat16)
    partial_sum = jnp.dot(genotypes, scaled, preferred_element_type=jnp.float32)
    phenotype = lax.psum(partial_sum, "mrk")
    standard = standardize(phenotype, samples)
    root_count = math.sqrt(samples)
    pieces = []
    for block_index in range(NBLK):
        columns = genotypes[:, block_index * BLK_DEV : (block_index + 1) * BLK_DEV]
        pieces.append(
            lax.psum_scatter(
                lax.dot_general(
                    standard, columns, (((0,), (0,)), ((), ())), preferred_element_type=jnp.float32
                ),
                "smp",
                scatter_dimension=0,
                tiled=True,
            )
        )
    summed = jnp.concatenate(pieces, axis=1)
    return summed * inverse_spread[None, :] / root_count


def solution(mesh):
    return jax.shard_map(
        shards,
        mesh=mesh,
        in_specs=(P("smp", ("grp", "mrk")), P(("grp", "mrk")), P("grp", None)),
        out_specs=P("smp", ("grp", "mrk")),
        check_vma=False,
    )
```

profile of v0, /device:TPU:0, one launch (start us, length us, event | category | flops | bytes accessed | tf_op | source)
XLA Modules:
  0.0 166.8 jit_solution(4051340667754941652)
XLA Ops:
  6.5 0.0 copy-start
  6.5 0.0 copy-start.2
  6.5 0.0 all-reduce.2.cloned.1.call-start
  6.5 2.9 %convert_reduce_fusion = f32[2048]{0:T(1024)S(1)} fusion(bf16[1024,2048]{1,0:T(8,128)(2,1)} %param.3), kind=kLoop, calls=%fused_computation.1 | loop fusion | flops 4192256 | bytes 4202496 | tf_op jit(solution)/shard_map/reduce_sum | solution.py:13
  9.4 13.7 %psum.35 = f32[2048]{0:T(1024)S(1)} all-reduce(f32[2048]{0:T(1024)S(1)} %convert_reduce_fusion), channel_id=1, replica_groups=mesh['grp'=2,'smp'=4,'mrk'=4] {'smp'}, use_global_device_ids=true, to_apply=%region_1.0 | all-reduce | flops 2048 | bytes 16384 | tf_op jit(solution)/shard_map/psum | solution.py:14
  23.2 3.3 %fusion.1 = f32[2048]{0:T(1024)S(1)} fusion(bf16[1024,2048]{1,0:T(8,128)(2,1)} %param.3, f32[2048]{0:T(1024)S(1)} %broadcast_multiply_fusion), kind=kLoop, calls=%fused_computation.3 | loop fusion | flops 8386560 | bytes 4210688 | tf_op jit(solution)/shard_map/reduce_sum | solution.py:15
  26.5 8.5 %psum.36 = f32[2048]{0:T(1024)S(1)} all-reduce(f32[2048]{0:T(1024)S(1)} %fusion.1), channel_id=1, replica_groups=mesh['grp'=2,'smp'=4,'mrk'=4] {'smp'}, use_global_device_ids=true, to_apply=%region_3.0 | all-reduce | flops 2048 | bytes 16384 | tf_op jit(solution)/shard_map/psum | solution.py:16
  35.0 0.0 copy-done
  35.0 0.0 copy-done.2
  35.1 5.8 %convolution_bitcast_fusion = f32[1024,256]{0,1:T(8,128)} fusion(bf16[1024,2048]{1,0:T(8,128)(2,1)} %param.3, bf16[512,256]{1,0:T(8,128)(2,1)S(1)} %copy-done, s32[2048]{0:T(1024)S(1)} %copy-done.2, f32[2048]{0:T(1024)S(1)} %add_rsqrt_fusion), kind=kOutput, calls=%fused_computation.13 | convolution fusion | flops 1612709888 | bytes 5521408 | tf_op jit(solution)/shard_map/dot_general | solution.py:38
  40.8 0.0 all-reduce.2.cloned.1.call-update
  40.8 0.0 reduce-scatter.3.cloned.1.call-start
  40.9 36.1 %all-reduce.2.cloned.1.call-done = f32[1024,256]{0,1:T(8,128)} async-done(((f32[1024,256]{0,1:T(8,128)}), f32[1024,256]{0,1:T(8,128)}) %all-reduce.2.cloned.1.call-update) | async-done | bytes 1048592 | tf_op jit(solution)/shard_map/psum | solution.py:39
  77.0 0.0 copy-start.1
  77.0 1.4 reduce_sum.38
  78.4 11.7 %psum.38 = f32[256]{0:T(256)S(1)} all-reduce(f32[256]{0:T(256)S(1)} %reduce_sum.38), channel_id=1, replica_groups=mesh['grp'=2,'smp'=4,'mrk'=4] {'smp'}, use_global_device_ids=true, to_apply=%region_6.0 | all-reduce | flops 256 | bytes 2048 | tf_op jit(solution)/shard_map/psum | solution.py:22
  90.1 1.5 multiply_reduce_fusion
  91.6 8.4 %psum.39 = f32[256]{0:T(256)S(1)} all-reduce(f32[256]{0:T(256)S(1)} %multiply_reduce_fusion), channel_id=1, replica_groups=mesh['grp'=2,'smp'=4,'mrk'=4] {'smp'}, use_global_device_ids=true, to_apply=%region_8.0 | all-reduce | flops 256 | bytes 2048 | tf_op jit(solution)/shard_map/psum | solution.py:24
  100.0 3.7 %fusion.7 = f32[256,1024]{1,0:T(8,128)} fusion(bf16[1024,2048]{1,0:T(8,128)(2,1)} %param.3, f32[1024,256]{0,1:T(8,128)} %all-reduce.2.cloned.1.call-done, f32[256]{0:T(256)S(1)} %add_rsqrt_fusion.1, f32[256]{0:T(256)S(1)} %broadcast_multiply_fusion.1), kind=kOutput, calls=%fused_computation.10 | convolution fusion | flops 537657344 | bytes 4196352 | tf_op jit(solution)/shard_map/dot_general | solution.py:47
  103.6 0.0 reduce-scatter.3.cloned.1.call-update
  103.7 0.0 reduce-scatter.5.cloned.1.call-start
  103.7 0.0 copy-done.1
  103.7 3.4 %fusion.5 = f32[256,1024]{1,0:T(8,128)} fusion(bf16[1024,2048]{1,0:T(8,128)(2,1)} %param.3, f32[1024,256]{0,1:T(8,128)S(1)} %copy-done.1, f32[256]{0:T(256)S(1)} %add_rsqrt_fusion.1, f32[256]{0:T(256)S(1)} %broadcast_multiply_fusion.1), kind=kOutput, calls=%fused_computation.8 | convolution fusion | flops 537657344 | bytes 4196352 | tf_op jit(solution)/shard_map/dot_general | solution.py:47
  107.1 0.0 reduce-scatter.5.cloned.1.call-update
  107.1 23.1 %reduce-scatter.3.cloned.1.call-done = f32[64,1024]{1,0:T(8,128)} async-done(((f32[256,1024]{1,0:T(8,128)}), f32[64,1024]{1,0:T(8,128)}) %reduce-scatter.3.cloned.1.call-update) | async-done | bytes 262160 | tf_op jit(solution)/shard_map/reduce_scatter | solution.py:46
  130.3 28.1 %reduce-scatter.5.cloned.1.call-done = f32[64,1024]{1,0:T(8,128)} async-done(((f32[256,1024]{1,0:T(8,128)}), f32[64,1024]{1,0:T(8,128)}) %reduce-scatter.5.cloned.1.call-update) | async-done | bytes 262160 | tf_op jit(solution)/shard_map/reduce_scatter | solution.py:46
  158.4 1.9 %fusion.10 = f32[64,2048]{1,0:T(8,128)} fusion(f32[64,1024]{1,0:T(8,128)} %reduce-scatter.5.cloned.1.call-done, f32[64,1024]{1,0:T(8,128)} %reduce-scatter.3.cloned.1.call-done, f32[2048]{0:T(1024)S(1)} %add_rsqrt_fusion), kind=kLoop, calls=%fused_computation.17 | loop fusion | flops 393216 | bytes 1056768 | tf_op jit(solution)/shard_map/div | solution.py:56
  (4 shorter events, 0.0 us)
Async XLA Ops:
  6.5 28.5 %copy-start = (bf16[512,256]{1,0:T(8,128)(2,1)S(1)}, bf16[512,256]{1,0:T(8,128)(2,1)}, u32[]{:S(2)}) copy-start(bf16[512,256]{1,0:T(8,128)(2,1)} %param.5) | copy-start | bytes 786436
  6.5 28.5 %copy-start.2 = (s32[2048]{0:T(1024)S(1)}, s32[2048]{0:T(1024)}, u32[]{:S(2)}) copy-start(s32[2048]{0:T(1024)} %param.4) | copy-start | bytes 24580
  6.5 70.4 %all-reduce.2.cloned.1.call-start = ((), (), s32[]{:S(2)}) async-start(), calls=%async_computation.2 | async-start | bytes 2097152 | tf_op jit(solution)/shard_map/psum | solution.py:39
  40.8 89.4 %reduce-scatter.3.cloned.1.call-start = ((), (), s32[]{:S(2)}) async-start(), calls=%async_computation.3 | async-start | bytes 1310720 | tf_op jit(solution)/shard_map/reduce_scatter | solution.py:46
  77.0 26.8 %copy-start.1 = (f32[1024,256]{0,1:T(8,128)S(1)}, f32[1024,256]{0,1:T(8,128)}, u32[]{:S(2)}) copy-start(f32[1024,256]{0,1:T(8,128)} %all-reduce.2.cloned.1.call-done) | copy-start | bytes 3145732
  103.7 54.7 %reduce-scatter.5.cloned.1.call-start = ((), (), s32[]{:S(2)}) async-start(), calls=%async_computation.4 | async-start | bytes 1310720 | tf_op jit(solution)/shard_map/reduce_scatter | solution.py:46
Sparse Core Ops, SparseCore 0:
  41.0 35.9 all-reduce.1
  103.8 26.4 reduce-scatter.2
  132.6 25.7 reduce-scatter.4
where the time goes:
time: 167 us
  waiting for transfers between devices  87.4 us (52%)
  blocking collectives  42.3 us (25%)
  between operations  13.2 us (8%)
  matrix products  12.8 us (8%)
  other arithmetic  11 us (7%)
    reduce_scatter x2, waiting for transfers between devices, shards(): lax.psum_scatter(lax.dot_general(standard, columns, (((0,), (0,)), ((), (...  51.3 us
    psum x1, waiting for transfers between devices, shards(): phenotype = lax.psum(partial_sum, 'mrk')  36.1 us
    psum x1, blocking collectives, marker_moments(): center = lax.psum(totals, 'smp') / samples  13.7 us
    psum x1, blocking collectives, standardize(): center = lax.psum(totals, 'smp') / samples  11.7 us
    psum x1, blocking collectives, marker_moments(): spread = lax.psum(local_squares, 'smp') / samples  8.51 us
    psum x1, blocking collectives, standardize(): spread = lax.psum(local_squares, 'smp') / samples  8.37 us
    dot_general x2, matrix products, shards(): lax.dot_general(standard, columns, (((0,), (0,)), ((), ())), preferred_el...  7.07 us
    dot_general x1, matrix products, shards(): partial_sum = jnp.dot(genotypes, scaled, preferred_element_type=jnp.float32)  5.77 us
  transfers between devices with their start and end apart: 3, of which 3 were waited for; matrix products, arithmetic and copies ran while one was open for 2% of the time, Pallas kernels for 0%

commit v1 on v0

--- a/solution.py
+++ b/solution.py
@@ -13,7 +13,7 @@
     totals = jnp.sum(genotypes, axis=0, dtype=jnp.float32)
     center = lax.psum(totals, "smp") / samples
     local_squares = jnp.sum(jnp.square(genotypes.astype(jnp.float32) - center[None, :]), axis=0)
-    spread = lax.psum(local_squares, "smp") / samples
+    spread = jnp.sum(lax.all_gather(local_squares, "smp"), axis=0) / samples
     return lax.rsqrt(spread + EPSILON)
 
 

time: 167 us -> 170 us (1.018)
  blocking collectives: 42.3 us -> 46.9 us
    all_gather x0 -> x1, blocking collectives: none -> 13.1 us  [marker_moments(): spread = jnp.sum(lax.all_gather(local_squares, 'smp'), axis=0) / samples]
    psum x1 -> x0, blocking collectives: 8.51 us -> none  [marker_moments(): spread = lax.psum(local_squares, 'smp') / samples]
where the time goes in v1:
time: 170 us
  waiting for transfers between devices  85.9 us (51%)
  blocking collectives  46.9 us (28%)
  between operations  13.2 us (8%)
  matrix products  12.8 us (8%)
  other arithmetic  11 us (6%)
    reduce_scatter x2, waiting for transfers between devices, shards(): lax.psum_scatter(lax.dot_general(standard, columns, (((0,), (0,)), ((), (...  51.3 us
    psum x1, waiting for transfers between devices, shards(): phenotype = lax.psum(partial_sum, 'mrk')  34.6 us
    psum x1, blocking collectives, marker_moments(): center = lax.psum(totals, 'smp') / samples  13.7 us
    all_gather x1, blocking collectives, marker_moments(): spread = jnp.sum(lax.all_gather(local_squares, 'smp'), axis=0) / samples  13.1 us
    psum x1, blocking collectives, standardize(): center = lax.psum(totals, 'smp') / samples  11.7 us
    psum x1, blocking collectives, standardize(): spread = lax.psum(local_squares, 'smp') / samples  8.37 us
    dot_general x2, matrix products, shards(): lax.dot_general(standard, columns, (((0,), (0,)), ((), ())), preferred_el...  7.07 us
    dot_general x1, matrix products, shards(): partial_sum = jnp.dot(genotypes, scaled, preferred_element_type=jnp.float32)  5.77 us
  transfers between devices with their start and end apart: 3, of which 3 were waited for; matrix products, arithmetic and copies ran while one was open for 2% of the time, Pallas kernels for 0%

profile of v1, /device:TPU:0, one launch (start us, length us, event | category | flops | bytes accessed | tf_op | source)
XLA Modules:
  0.0 170.0 jit_solution(1480987931171910487)
XLA Ops:
  6.5 0.0 copy-start
  6.5 0.0 copy-start.2
  6.5 0.0 all-reduce.2.cloned.1.call-start
  6.5 2.9 %convert_reduce_fusion = f32[2048]{0:T(1024)S(1)} fusion(bf16[1024,2048]{1,0:T(8,128)(2,1)} %param.3), kind=kLoop, calls=%fused_computation.1 | loop fusion | flops 4192256 | bytes 4202496 | tf_op jit(solution)/shard_map/reduce_sum | solution.py:13
  9.4 13.7 %psum.28 = f32[2048]{0:T(1024)S(1)} all-reduce(f32[2048]{0:T(1024)S(1)} %convert_reduce_fusion), channel_id=1, replica_groups=mesh['grp'=2,'smp'=4,'mrk'=4] {'smp'}, use_global_device_ids=true, to_apply=%region_1.0 | all-reduce | flops 2048 | bytes 16384 | tf_op jit(solution)/shard_map/psum | solution.py:14
  23.2 3.3 %fusion.1 = f32[2048]{0:T(1024)S(1)} fusion(bf16[1024,2048]{1,0:T(8,128)(2,1)} %param.3, f32[2048]{0:T(1024)S(1)} %broadcast_multiply_fusion), kind=kLoop, calls=%fused_computation.3 | loop fusion | flops 8386560 | bytes 4210688 | tf_op jit(solution)/shard_map/reduce_sum | solution.py:15
  26.5 13.1 %all-gather = f32[8192]{0:T(1024)S(1)} all-gather(f32[2048]{0:T(1024)S(1)} %fusion.1), channel_id=2, replica_groups=mesh['grp'=2,'smp'=4,'mrk'=4] {'smp'}, dimensions={0}, use_global_device_ids=true | all-gather | bytes 40960 | tf_op jit(solution)/shard_map/all_gather | solution.py:16
  39.7 0.0 copy-done
  39.7 0.0 copy-done.2
  39.7 5.8 %convolution_bitcast_fusion = f32[1024,256]{0,1:T(8,128)} fusion(bf16[1024,2048]{1,0:T(8,128)(2,1)} %param.3, bf16[512,256]{1,0:T(8,128)(2,1)S(1)} %copy-done, s32[2048]{0:T(1024)S(1)} %copy-done.2, f32[2048]{0:T(1024)S(1)} %add_rsqrt_fusion), kind=kOutput, calls=%fused_computation.13 | convolution fusion | flops 1612709888 | bytes 5521408 | tf_op jit(solution)/shard_map/dot_general | solution.py:38
  45.5 0.0 all-reduce.2.cloned.1.call-update
  45.5 0.0 reduce-scatter.3.cloned.1.call-start
  45.6 34.6 %all-reduce.2.cloned.1.call-done = f32[1024,256]{0,1:T(8,128)} async-done(((f32[1024,256]{0,1:T(8,128)}), f32[1024,256]{0,1:T(8,128)}) %all-reduce.2.cloned.1.call-update) | async-done | bytes 1048592 | tf_op jit(solution)/shard_map/psum | solution.py:39
  80.2 0.0 copy-start.1
  80.2 1.4 reduce_sum.48
  81.6 11.7 %psum.30 = f32[256]{0:T(256)S(1)} all-reduce(f32[256]{0:T(256)S(1)} %reduce_sum.48), channel_id=1, replica_groups=mesh['grp'=2,'smp'=4,'mrk'=4] {'smp'}, use_global_device_ids=true, to_apply=%region_6.0 | all-reduce | flops 256 | bytes 2048 | tf_op jit(solution)/shard_map/psum | solution.py:22
  93.3 1.5 multiply_reduce_fusion
  94.8 8.4 %psum.31 = f32[256]{0:T(256)S(1)} all-reduce(f32[256]{0:T(256)S(1)} %multiply_reduce_fusion), channel_id=1, replica_groups=mesh['grp'=2,'smp'=4,'mrk'=4] {'smp'}, use_global_device_ids=true, to_apply=%region_8.0 | all-reduce | flops 256 | bytes 2048 | tf_op jit(solution)/shard_map/psum | solution.py:24
  103.2 3.7 %fusion.7 = f32[256,1024]{1,0:T(8,128)} fusion(bf16[1024,2048]{1,0:T(8,128)(2,1)} %param.3, f32[1024,256]{0,1:T(8,128)} %all-reduce.2.cloned.1.call-done, f32[256]{0:T(256)S(1)} %add_rsqrt_fusion.1, f32[256]{0:T(256)S(1)} %broadcast_multiply_fusion.1), kind=kOutput, calls=%fused_computation.10 | convolution fusion | flops 537657344 | bytes 4196352 | tf_op jit(solution)/shard_map/dot_general | solution.py:47
  106.9 0.0 reduce-scatter.3.cloned.1.call-update
  106.9 0.0 reduce-scatter.5.cloned.1.call-start
  106.9 0.0 copy-done.1
  106.9 3.4 %fusion.5 = f32[256,1024]{1,0:T(8,128)} fusion(bf16[1024,2048]{1,0:T(8,128)(2,1)} %param.3, f32[1024,256]{0,1:T(8,128)S(1)} %copy-done.1, f32[256]{0:T(256)S(1)} %add_rsqrt_fusion.1, f32[256]{0:T(256)S(1)} %broadcast_multiply_fusion.1), kind=kOutput, calls=%fused_computation.8 | convolution fusion | flops 537657344 | bytes 4196352 | tf_op jit(solution)/shard_map/dot_general | solution.py:47
  110.3 0.0 reduce-scatter.5.cloned.1.call-update
  110.4 23.1 %reduce-scatter.3.cloned.1.call-done = f32[64,1024]{1,0:T(8,128)} async-done(((f32[256,1024]{1,0:T(8,128)}), f32[64,1024]{1,0:T(8,128)}) %reduce-scatter.3.cloned.1.call-update) | async-done | bytes 262160 | tf_op jit(solution)/shard_map/reduce_scatter | solution.py:46
  133.5 28.1 %reduce-scatter.5.cloned.1.call-done = f32[64,1024]{1,0:T(8,128)} async-done(((f32[256,1024]{1,0:T(8,128)}), f32[64,1024]{1,0:T(8,128)}) %reduce-scatter.5.cloned.1.call-update) | async-done | bytes 262160 | tf_op jit(solution)/shard_map/reduce_scatter | solution.py:46
  161.6 1.9 %fusion.10 = f32[64,2048]{1,0:T(8,128)} fusion(f32[64,1024]{1,0:T(8,128)} %reduce-scatter.5.cloned.1.call-done, f32[64,1024]{1,0:T(8,128)} %reduce-scatter.3.cloned.1.call-done, f32[2048]{0:T(1024)S(1)} %add_rsqrt_fusion), kind=kLoop, calls=%fused_computation.17 | loop fusion | flops 393216 | bytes 1056768 | tf_op jit(solution)/shard_map/div | solution.py:56
  (6 shorter events, 0.1 us)
Async XLA Ops:
  6.5 33.2 %copy-start = (bf16[512,256]{1,0:T(8,128)(2,1)S(1)}, bf16[512,256]{1,0:T(8,128)(2,1)}, u32[]{:S(2)}) copy-start(bf16[512,256]{1,0:T(8,128)(2,1)} %param.5) | copy-start | bytes 786436
  6.5 33.2 %copy-start.2 = (s32[2048]{0:T(1024)S(1)}, s32[2048]{0:T(1024)}, u32[]{:S(2)}) copy-start(s32[2048]{0:T(1024)} %param.4) | copy-start | bytes 24580
  6.5 73.6 %all-reduce.2.cloned.1.call-start = ((), (), s32[]{:S(2)}) async-start(), calls=%async_computation.2 | async-start | bytes 2097152 | tf_op jit(solution)/shard_map/psum | solution.py:39
  45.5 88.0 %reduce-scatter.3.cloned.1.call-start = ((), (), s32[]{:S(2)}) async-start(), calls=%async_computation.3 | async-start | bytes 1310720 | tf_op jit(solution)/shard_map/reduce_scatter | solution.py:46
  80.2 26.8 %copy-start.1 = (f32[1024,256]{0,1:T(8,128)S(1)}, f32[1024,256]{0,1:T(8,128)}, u32[]{:S(2)}) copy-start(f32[1024,256]{0,1:T(8,128)} %all-reduce.2.cloned.1.call-done) | copy-start | bytes 3145732
  106.9 54.7 %reduce-scatter.5.cloned.1.call-start = ((), (), s32[]{:S(2)}) async-start(), calls=%async_computation.4 | async-start | bytes 1310720 | tf_op jit(solution)/shard_map/reduce_scatter | solution.py:46
Sparse Core Ops, SparseCore 0:
  45.6 34.5 all-reduce.1
  107.0 26.4 reduce-scatter.2
  135.8 25.7 reduce-scatter.4
